TPU v7x, 32 devices: a whole 2x2x4 slice. The times are simulated.
32 devices in a mesh: db: 8 (over y, x, core), pb: 4 (over z).
Axes of the slice: x: 2, y: 2, z: 4, core: 2. Of those that a mesh axis runs over, the one named last changes fastest.
Arguments:
- query_maps: bfloat16 [32, 256, 256], P(('db', 'pb')), may hold values from -6 to 6
- database: bfloat16 [1024, 256, 256], P(('db', 'pb')), may hold values from -6 to 6
- shortlist: int32 [32, 128], P(('db', 'pb')), may hold values from 0 to 1023, as said below
- kernel_query: bfloat16 [3, 3], replicated, may hold values from -1.5 to 1.5
- kernel_db: bfloat16 [3, 3], replicated, may hold values from -1.5 to 1.5
Outputs:
- scores: float32 [32, 128], P(('db', 'pb'))
- top_scores: float32 [32, 100], P(('db', 'pb'))
Inputs may be any that keep to these rules, and one draw needn't show every extreme that they name: Within one query the ids are distinct. Among the 128 shortlist entries of the query held by device q (query q), at most 8 lie in any one shard of images (ids s * 32 to (s + 1) * 32 - 1), and some shard holds exactly 8 of them for every device.
All inputs are finite; a program needn't handle non-finite values.
Results may differ from a plain program's by a relative error of at most 0.0003.
Values may be sent and summed in bfloat16 or wider, within the bound.
A program may use at most 128 MiB of HBM per device.

v0:
```python
import math
import jax
import jax.numpy as jnp
from jax import lax
from jax.sharding import PartitionSpec as P

GRID = 16
TOPK = 100
epsilon = 1e-06
score_scale = 8.0


def unit_maps(maps):
    values = maps.astype(jnp.float32)
    squares = jnp.sum(values * values, axis=1, keepdims=True)
    return (values * lax.rsqrt(squares + epsilon)).astype(jnp.bfloat16)


def conv_matrix(kernel):
    cell_count = GRID * GRID
    cell_index = jnp.arange(cell_count)
    row_out = (cell_index // GRID)[:, None]
    col_out = (cell_index % GRID)[:, None]
    row_in = (cell_index // GRID)[None, :]
    col_in = (cell_index % GRID)[None, :]
    weights = kernel.astype(jnp.float32)
    matrix = jnp.zeros((cell_count, cell_count), jnp.float32)
    for i in range(3):
        for j in range(3):
            hit = (row_in == row_out + i - 1) & (col_in == col_out + j - 1)
            matrix = matrix + weights[i, j] * hit.astype(jnp.float32)
    return matrix.astype(jnp.bfloat16)


def finish_pairs(correlation, conv_query, conv_db):
    rectified = jnp.maximum(correlation, 0.0).astype(jnp.bfloat16)
    filtered = jnp.einsum("qa,nab->nqb", conv_query, rectified, preferred_element_type=jnp.float32)
    filtered = filtered + jnp.einsum(
        "nqa,ba->nqb", rectified, conv_db, preferred_element_type=jnp.float32
    )
    return score_scale * jnp.mean(jnp.max(filtered, axis=1), axis=-1)


def shard_scores(gathered, slots, db_unit, conv_query, conv_db):
    source_count, width = slots.shape
    per_query = gathered.shape[0] // source_count
    grouped = gathered.reshape(source_count, per_query, gathered.shape[1], gathered.shape[2])
    step_size = math.gcd(source_count, max(1, 32 // width))

    def score_block(start):
        slot_block = lax.dynamic_slice_in_dim(slots, start, step_size, 0)
        group_block = lax.dynamic_slice_in_dim(grouped, start, step_size, 0)
        images = db_unit[slot_block]
        correlation = jnp.einsum(
            "scq,skcd->skqd", group_block[:, 0], images, preferred_element_type=jnp.float32
        )
        correlation = correlation.reshape(
            step_size * width, correlation.shape[-2], correlation.shape[-1]
        )
        return finish_pairs(correlation, conv_query, conv_db)

    starts = jnp.arange(source_count // step_size, dtype=jnp.int32) * step_size
    return lax.map(score_block, starts).reshape(source_count, width)


def body(query_maps, database, shortlist, kernel_query, kernel_db):
    query_unit = unit_maps(query_maps)
    db_unit = unit_maps(database)
    conv_query = conv_matrix(kernel_query)
    conv_db = conv_matrix(kernel_db)
    db_count = lax.axis_size("db")
    pb_count = lax.axis_size("pb")
    shard_count = db_count * pb_count
    per_query = query_maps.shape[0]
    cand_count = shortlist.shape[1]
    image_count = database.shape[0]
    flat_ids = shortlist.reshape(-1)
    row_count = flat_ids.shape[0]
    capacity = 2 * row_count // shard_count
    shard_of = flat_ids // image_count
    slot_of = flat_ids % image_count
    one_hot = (shard_of[:, None] == jnp.arange(shard_count, dtype=jnp.int32)[None, :]).astype(
        jnp.int32
    )
    bucket_pos = jnp.sum(jnp.cumsum(one_hot, axis=0) * one_hot, axis=1) - 1
    row_ids = jnp.arange(row_count, dtype=jnp.int32)
    query_of = row_ids // cand_count
    empty = jnp.zeros((shard_count, capacity), jnp.int32)
    send_slot = empty.at[shard_of, bucket_pos].set(slot_of)
    send_query = empty.at[shard_of, bucket_pos].set(query_of)
    requests = jnp.stack([send_slot, send_query])
    gathered = lax.all_gather(query_unit, ("db", "pb"), axis=0, tiled=True)
    found = shard_scores(
        gathered,
        lax.all_to_all(requests, ("db", "pb"), split_axis=1, concat_axis=1, tiled=True)[0],
        db_unit,
        conv_query,
        conv_db,
    )
    returned = lax.all_to_all(found, ("db", "pb"), split_axis=0, concat_axis=0, tiled=True)
    scores = returned[shard_of, bucket_pos].reshape(per_query, cand_count)
    top_scores = lax.top_k(scores, TOPK)[0]
    return (scores, top_scores)


def solution(mesh):
    in_specs = (
        P(("db", "pb"), None, None),
        P(("db", "pb"), None, None),
        P(("db", "pb"), None),
        P(),
        P(),
    )
    out_specs = (P(("db", "pb"), None), P(("db", "pb"), None))
    return jax.shard_map(body, mesh=mesh, in_specs=in_specs, out_specs=out_specs, check_vma=False)
```

profile of v0, /device:TPU:0, one launch (start us, length us, event | category | flops | bytes accessed | tf_op | source)
XLA Modules:
  0.0 317.0 jit_solution(1332410492687568349)
XLA Ops:
  7.2 1.0 fusion.53
  8.2 1.6 fusion.54
  9.8 0.7 and_select_fusion.3
  10.5 0.2 reduce_window_sum.11
  10.7 0.2 select_reduce_fusion
  10.9 0.7 fusion.61
  11.6 6.4 %scatter_fusion = s32[32,8]{0,1:T(8,128)S(1)} fusion(s32[32,8]{0,1:T(8,128)S(1)} %broadcast_in_dim.11.clone.1, s32[128]{0:T(128)S(1)} %fusion.60, s32[128]{0:T(128)S(1)} %get-tuple-element.427), kind=kCustom, calls=%fused_computation.2 | custom fusion | bytes 2560 | tf_op jit(solution)/shard_map/scatter | solution.py:89
  18.1 6.4 %scatter_fusion.1 = s32[32,8]{0,1:T(8,128)S(1)} fusion(s32[32,8]{0,1:T(8,128)S(1)} %broadcast_in_dim.11.clone, s32[128]{0:T(128)S(1)} %fusion.60, s32[128]{0:T(128)S(1)} %and_select_fusion.2), kind=kCustom, calls=%fused_computation.3 | custom fusion | bytes 2560 | tf_op jit(solution)/shard_map/scatter | solution.py:90
  24.5 0.7 copy.23
  25.2 7.3 %all-to-all-start = ((s32[2,32,8]{2,0,1:T(2,128)}), s32[2,32,8]{2,0,1:T(2,128)S(1)}, u32[]{:S(2)}, u32[]{:S(2)}) async-start(s32[2,32,8]{2,0,1:T(2,128)} %copy.23), calls=%async_computation | async-start | bytes 65536 | tf_op jit(solution)/shard_map/all_to_all | solution.py:95
  32.6 1.7 fusion.63
  34.3 1.7 fusion.62
  36.0 3.1 fusion.51
  39.1 3.1 fusion.52
  42.2 33.2 %all-gather.2.cloned.1.call-done = bf16[32,256,256]{2,1,0:T(8,128)(2,1)} async-done(((bf16[1,256,256]{2,1,0:T(8,128)(2,1)}), bf16[32,256,256]{2,1,0:T(8,128)(2,1)}) %all-gather.2.cloned.1.call-update) | async-done | bytes 4194320 | tf_op jit(solution)/shard_map/all_gather | solution.py:92
  75.4 220.3 %while.14 = (s32[]{:T(128)}, f32[8,32]{1,0:T(8,128)S(1)}, s32[8]{0:T(128)S(1)}, s32[32,8]{1,0:T(8,128)S(1)}, bf16[32,256,256]{2,1,0:T(8,128)(2,1)}, /*index=5*/b...) while((s32[]{:T(128)}, f32[8,32]{1,0:T(8,128)S(1)}, ...), condition=%wide.region_9.10_spmd.clone.clone, body=%wide.region_6.9_spmd.clone.clone.sunk | while | flops 3233940480 | bytes 42551080 | solution.py:63
  75.4 0.6 dynamic_slice.35
  77.8 5.0 %gather_fusion = bf16[32,256,256]{2,1,0:T(8,128)(2,1)} fusion(bf16[32,256,256]{2,1,0:T(8,128)(2,1)} %get-tuple-element.688, s32[1024]{0:T(1024)S(1)} %pad_clamp_fusion.2), kind=kCustom, calls=%fused_computation.clone.clone.clone.1 | custom fusion | bytes 8388736 | tf_op jit(solution)/shard_map/while/body/eval_jaxpr/gather | solution.py:53
  82.7 4.0 %maximum_convert_fusion.2 = bf16[4,8,256,256]{3,2,1,0:T(8,128)(2,1)S(1)} fusion(bf16[4,8,256,256]{3,2,1,0:T(8,128)(2,1)} %bitcast.126, bf16[32,1,256,256]{3,2,0,1:T(8,128)(2,1)} %get-tuple-element.689, s32[]{:T(128)S(6)} %select_n.224), kind=kOutput, calls=%fused_computation.8.clone.1 | convolution fusion | flops 1077936128 | bytes 8912900 | tf_op jit(solution)/shard_map/while/body/eval_jaxpr/scq,skcd->skqd/dot_general | solution.py:54
  86.8 7.3 %fusion.81 = f32[32,256,256]{1,2,0:T(8,128)S(1)} fusion(bf16[32,256,256]{1,2,0:T(8,128)(2,1)S(1)} %bitcast.124, f32[]{:T(128)} %get-tuple-element.704, f32[]{:T(128)} %get-tuple-element.701, f32[]{:T(128)} %get-tuple-element.699, f32[]{:T(128)} %get-tuple-element.697, f32[]{:T(128)} %get-tuple-element.695, f32[]{:T(128)} %get-tuple-element.694, ...), kind=kOutput, calls=%fused_computation.23.clone.1 | convolution fusion | flops 1075904512 | bytes 12589092 | tf_op jit(solution)/shard_map/while/body/eval_jaxpr/qa,nab->nqb/dot_general | solution.py:37
  94.1 8.6 %fusion.82 = f32[32,256]{1,0:T(8,128)S(1)} fusion(f32[32,256,256]{1,2,0:T(8,128)S(1)} %fusion.81, bf16[32,256,256]{1,2,0:T(8,128)(2,1)S(1)} %bitcast.125, f32[]{:T(128)} %get-tuple-element.713, f32[]{:T(128)} %get-tuple-element.712, f32[]{:T(128)} %get-tuple-element.711, f32[]{:T(128)} %get-tuple-element.710, f32[]{:T(128)} %get-tuple-element.709, ...), kind=kOutput, calls=%fused_computation.7.clone.1 | convolution fusion | flops 1080090624 | bytes 12621860 | tf_op jit(solution)/shard_map/while/body/eval_jaxpr/nqa,ba->nqb/dot_general | solution.py:38
  102.7 0.1 reduce_sum.48
  102.9 0.6 dynamic_slice.35
  105.3 5.0 %gather_fusion = bf16[32,256,256]{2,1,0:T(8,128)(2,1)} fusion(bf16[32,256,256]{2,1,0:T(8,128)(2,1)} %get-tuple-element.688, s32[1024]{0:T(1024)S(1)} %pad_clamp_fusion.2), kind=kCustom, calls=%fused_computation.clone.clone.clone.1 | custom fusion | bytes 8388736 | tf_op jit(solution)/shard_map/while/body/eval_jaxpr/gather | solution.py:53
  110.3 4.0 %maximum_convert_fusion.2 = bf16[4,8,256,256]{3,2,1,0:T(8,128)(2,1)S(1)} fusion(bf16[4,8,256,256]{3,2,1,0:T(8,128)(2,1)} %bitcast.126, bf16[32,1,256,256]{3,2,0,1:T(8,128)(2,1)} %get-tuple-element.689, s32[]{:T(128)S(6)} %select_n.224), kind=kOutput, calls=%fused_computation.8.clone.1 | convolution fusion | flops 1077936128 | bytes 8912900 | tf_op jit(solution)/shard_map/while/body/eval_jaxpr/scq,skcd->skqd/dot_general | solution.py:54
  114.3 7.3 %fusion.81 = f32[32,256,256]{1,2,0:T(8,128)S(1)} fusion(bf16[32,256,256]{1,2,0:T(8,128)(2,1)S(1)} %bitcast.124, f32[]{:T(128)} %get-tuple-element.704, f32[]{:T(128)} %get-tuple-element.701, f32[]{:T(128)} %get-tuple-element.699, f32[]{:T(128)} %get-tuple-element.697, f32[]{:T(128)} %get-tuple-element.695, f32[]{:T(128)} %get-tuple-element.694, ...), kind=kOutput, calls=%fused_computation.23.clone.1 | convolution fusion | flops 1075904512 | bytes 12589092 | tf_op jit(solution)/shard_map/while/body/eval_jaxpr/qa,nab->nqb/dot_general | solution.py:37
  121.6 8.6 %fusion.82 = f32[32,256]{1,0:T(8,128)S(1)} fusion(f32[32,256,256]{1,2,0:T(8,128)S(1)} %fusion.81, bf16[32,256,256]{1,2,0:T(8,128)(2,1)S(1)} %bitcast.125, f32[]{:T(128)} %get-tuple-element.713, f32[]{:T(128)} %get-tuple-element.712, f32[]{:T(128)} %get-tuple-element.711, f32[]{:T(128)} %get-tuple-element.710, f32[]{:T(128)} %get-tuple-element.709, ...), kind=kOutput, calls=%fused_computation.7.clone.1 | convolution fusion | flops 1080090624 | bytes 12621860 | tf_op jit(solution)/shard_map/while/body/eval_jaxpr/nqa,ba->nqb/dot_general | solution.py:38
  130.3 0.1 reduce_sum.48
  130.5 0.6 dynamic_slice.35
  132.8 5.0 %gather_fusion = bf16[32,256,256]{2,1,0:T(8,128)(2,1)} fusion(bf16[32,256,256]{2,1,0:T(8,128)(2,1)} %get-tuple-element.688, s32[1024]{0:T(1024)S(1)} %pad_clamp_fusion.2), kind=kCustom, calls=%fused_computation.clone.clone.clone.1 | custom fusion | bytes 8388736 | tf_op jit(solution)/shard_map/while/body/eval_jaxpr/gather | solution.py:53
  137.8 4.0 %maximum_convert_fusion.2 = bf16[4,8,256,256]{3,2,1,0:T(8,128)(2,1)S(1)} fusion(bf16[4,8,256,256]{3,2,1,0:T(8,128)(2,1)} %bitcast.126, bf16[32,1,256,256]{3,2,0,1:T(8,128)(2,1)} %get-tuple-element.689, s32[]{:T(128)S(6)} %select_n.224), kind=kOutput, calls=%fused_computation.8.clone.1 | convolution fusion | flops 1077936128 | bytes 8912900 | tf_op jit(solution)/shard_map/while/body/eval_jaxpr/scq,skcd->skqd/dot_general | solution.py:54
  141.8 7.3 %fusion.81 = f32[32,256,256]{1,2,0:T(8,128)S(1)} fusion(bf16[32,256,256]{1,2,0:T(8,128)(2,1)S(1)} %bitcast.124, f32[]{:T(128)} %get-tuple-element.704, f32[]{:T(128)} %get-tuple-element.701, f32[]{:T(128)} %get-tuple-element.699, f32[]{:T(128)} %get-tuple-element.697, f32[]{:T(128)} %get-tuple-element.695, f32[]{:T(128)} %get-tuple-element.694, ...), kind=kOutput, calls=%fused_computation.23.clone.1 | convolution fusion | flops 1075904512 | bytes 12589092 | tf_op jit(solution)/shard_map/while/body/eval_jaxpr/qa,nab->nqb/dot_general | solution.py:37
  149.2 8.6 %fusion.82 = f32[32,256]{1,0:T(8,128)S(1)} fusion(f32[32,256,256]{1,2,0:T(8,128)S(1)} %fusion.81, bf16[32,256,256]{1,2,0:T(8,128)(2,1)S(1)} %bitcast.125, f32[]{:T(128)} %get-tuple-element.713, f32[]{:T(128)} %get-tuple-element.712, f32[]{:T(128)} %get-tuple-element.711, f32[]{:T(128)} %get-tuple-element.710, f32[]{:T(128)} %get-tuple-element.709, ...), kind=kOutput, calls=%fused_computation.7.clone.1 | convolution fusion | flops 1080090624 | bytes 12621860 | tf_op jit(solution)/shard_map/while/body/eval_jaxpr/nqa,ba->nqb/dot_general | solution.py:38
  157.8 0.1 reduce_sum.48
  158.0 0.6 dynamic_slice.35
  160.4 5.0 %gather_fusion = bf16[32,256,256]{2,1,0:T(8,128)(2,1)} fusion(bf16[32,256,256]{2,1,0:T(8,128)(2,1)} %get-tuple-element.688, s32[1024]{0:T(1024)S(1)} %pad_clamp_fusion.2), kind=kCustom, calls=%fused_computation.clone.clone.clone.1 | custom fusion | bytes 8388736 | tf_op jit(solution)/shard_map/while/body/eval_jaxpr/gather | solution.py:53
  165.4 4.0 %maximum_convert_fusion.2 = bf16[4,8,256,256]{3,2,1,0:T(8,128)(2,1)S(1)} fusion(bf16[4,8,256,256]{3,2,1,0:T(8,128)(2,1)} %bitcast.126, bf16[32,1,256,256]{3,2,0,1:T(8,128)(2,1)} %get-tuple-element.689, s32[]{:T(128)S(6)} %select_n.224), kind=kOutput, calls=%fused_computation.8.clone.1 | convolution fusion | flops 1077936128 | bytes 8912900 | tf_op jit(solution)/shard_map/while/body/eval_jaxpr/scq,skcd->skqd/dot_general | solution.py:54
  169.4 7.3 %fusion.81 = f32[32,256,256]{1,2,0:T(8,128)S(1)} fusion(bf16[32,256,256]{1,2,0:T(8,128)(2,1)S(1)} %bitcast.124, f32[]{:T(128)} %get-tuple-element.704, f32[]{:T(128)} %get-tuple-element.701, f32[]{:T(128)} %get-tuple-element.699, f32[]{:T(128)} %get-tuple-element.697, f32[]{:T(128)} %get-tuple-element.695, f32[]{:T(128)} %get-tuple-element.694, ...), kind=kOutput, calls=%fused_computation.23.clone.1 | convolution fusion | flops 1075904512 | bytes 12589092 | tf_op jit(solution)/shard_map/while/body/eval_jaxpr/qa,nab->nqb/dot_general | solution.py:37
  176.7 8.6 %fusion.82 = f32[32,256]{1,0:T(8,128)S(1)} fusion(f32[32,256,256]{1,2,0:T(8,128)S(1)} %fusion.81, bf16[32,256,256]{1,2,0:T(8,128)(2,1)S(1)} %bitcast.125, f32[]{:T(128)} %get-tuple-element.713, f32[]{:T(128)} %get-tuple-element.712, f32[]{:T(128)} %get-tuple-element.711, f32[]{:T(128)} %get-tuple-element.710, f32[]{:T(128)} %get-tuple-element.709, ...), kind=kOutput, calls=%fused_computation.7.clone.1 | convolution fusion | flops 1080090624 | bytes 12621860 | tf_op jit(solution)/shard_map/while/body/eval_jaxpr/nqa,ba->nqb/dot_general | solution.py:38
  185.4 0.1 reduce_sum.48
  185.6 0.6 dynamic_slice.35
  187.9 5.0 %gather_fusion = bf16[32,256,256]{2,1,0:T(8,128)(2,1)} fusion(bf16[32,256,256]{2,1,0:T(8,128)(2,1)} %get-tuple-element.688, s32[1024]{0:T(1024)S(1)} %pad_clamp_fusion.2), kind=kCustom, calls=%fused_computation.clone.clone.clone.1 | custom fusion | bytes 8388736 | tf_op jit(solution)/shard_map/while/body/eval_jaxpr/gather | solution.py:53
  192.9 4.0 %maximum_convert_fusion.2 = bf16[4,8,256,256]{3,2,1,0:T(8,128)(2,1)S(1)} fusion(bf16[4,8,256,256]{3,2,1,0:T(8,128)(2,1)} %bitcast.126, bf16[32,1,256,256]{3,2,0,1:T(8,128)(2,1)} %get-tuple-element.689, s32[]{:T(128)S(6)} %select_n.224), kind=kOutput, calls=%fused_computation.8.clone.1 | convolution fusion | flops 1077936128 | bytes 8912900 | tf_op jit(solution)/shard_map/while/body/eval_jaxpr/scq,skcd->skqd/dot_general | solution.py:54
  196.9 7.3 %fusion.81 = f32[32,256,256]{1,2,0:T(8,128)S(1)} fusion(bf16[32,256,256]{1,2,0:T(8,128)(2,1)S(1)} %bitcast.124, f32[]{:T(128)} %get-tuple-element.704, f32[]{:T(128)} %get-tuple-element.701, f32[]{:T(128)} %get-tuple-element.699, f32[]{:T(128)} %get-tuple-element.697, f32[]{:T(128)} %get-tuple-element.695, f32[]{:T(128)} %get-tuple-element.694, ...), kind=kOutput, calls=%fused_computation.23.clone.1 | convolution fusion | flops 1075904512 | bytes 12589092 | tf_op jit(solution)/shard_map/while/body/eval_jaxpr/qa,nab->nqb/dot_general | solution.py:37
  204.3 8.6 %fusion.82 = f32[32,256]{1,0:T(8,128)S(1)} fusion(f32[32,256,256]{1,2,0:T(8,128)S(1)} %fusion.81, bf16[32,256,256]{1,2,0:T(8,128)(2,1)S(1)} %bitcast.125, f32[]{:T(128)} %get-tuple-element.713, f32[]{:T(128)} %get-tuple-element.712, f32[]{:T(128)} %get-tuple-element.711, f32[]{:T(128)} %get-tuple-element.710, f32[]{:T(128)} %get-tuple-element.709, ...), kind=kOutput, calls=%fused_computation.7.clone.1 | convolution fusion | flops 1080090624 | bytes 12621860 | tf_op jit(solution)/shard_map/while/body/eval_jaxpr/nqa,ba->nqb/dot_general | solution.py:38
  213.1 0.6 dynamic_slice.35
  215.5 5.0 %gather_fusion = bf16[32,256,256]{2,1,0:T(8,128)(2,1)} fusion(bf16[32,256,256]{2,1,0:T(8,128)(2,1)} %get-tuple-element.688, s32[1024]{0:T(1024)S(1)} %pad_clamp_fusion.2), kind=kCustom, calls=%fused_computation.clone.clone.clone.1 | custom fusion | bytes 8388736 | tf_op jit(solution)/shard_map/while/body/eval_jaxpr/gather | solution.py:53
  220.5 4.0 %maximum_convert_fusion.2 = bf16[4,8,256,256]{3,2,1,0:T(8,128)(2,1)S(1)} fusion(bf16[4,8,256,256]{3,2,1,0:T(8,128)(2,1)} %bitcast.126, bf16[32,1,256,256]{3,2,0,1:T(8,128)(2,1)} %get-tuple-element.689, s32[]{:T(128)S(6)} %select_n.224), kind=kOutput, calls=%fused_computation.8.clone.1 | convolution fusion | flops 1077936128 | bytes 8912900 | tf_op jit(solution)/shard_map/while/body/eval_jaxpr/scq,skcd->skqd/dot_general | solution.py:54
  224.5 7.3 %fusion.81 = f32[32,256,256]{1,2,0:T(8,128)S(1)} fusion(bf16[32,256,256]{1,2,0:T(8,128)(2,1)S(1)} %bitcast.124, f32[]{:T(128)} %get-tuple-element.704, f32[]{:T(128)} %get-tuple-element.701, f32[]{:T(128)} %get-tuple-element.699, f32[]{:T(128)} %get-tuple-element.697, f32[]{:T(128)} %get-tuple-element.695, f32[]{:T(128)} %get-tuple-element.694, ...), kind=kOutput, calls=%fused_computation.23.clone.1 | convolution fusion | flops 1075904512 | bytes 12589092 | tf_op jit(solution)/shard_map/while/body/eval_jaxpr/qa,nab->nqb/dot_general | solution.py:37
  231.8 8.6 %fusion.82 = f32[32,256]{1,0:T(8,128)S(1)} fusion(f32[32,256,256]{1,2,0:T(8,128)S(1)} %fusion.81, bf16[32,256,256]{1,2,0:T(8,128)(2,1)S(1)} %bitcast.125, f32[]{:T(128)} %get-tuple-element.713, f32[]{:T(128)} %get-tuple-element.712, f32[]{:T(128)} %get-tuple-element.711, f32[]{:T(128)} %get-tuple-element.710, f32[]{:T(128)} %get-tuple-element.709, ...), kind=kOutput, calls=%fused_computation.7.clone.1 | convolution fusion | flops 1080090624 | bytes 12621860 | tf_op jit(solution)/shard_map/while/body/eval_jaxpr/nqa,ba->nqb/dot_general | solution.py:38
  240.6 0.6 dynamic_slice.35
  243.0 5.0 %gather_fusion = bf16[32,256,256]{2,1,0:T(8,128)(2,1)} fusion(bf16[32,256,256]{2,1,0:T(8,128)(2,1)} %get-tuple-element.688, s32[1024]{0:T(1024)S(1)} %pad_clamp_fusion.2), kind=kCustom, calls=%fused_computation.clone.clone.clone.1 | custom fusion | bytes 8388736 | tf_op jit(solution)/shard_map/while/body/eval_jaxpr/gather | solution.py:53
  248.0 4.0 %maximum_convert_fusion.2 = bf16[4,8,256,256]{3,2,1,0:T(8,128)(2,1)S(1)} fusion(bf16[4,8,256,256]{3,2,1,0:T(8,128)(2,1)} %bitcast.126, bf16[32,1,256,256]{3,2,0,1:T(8,128)(2,1)} %get-tuple-element.689, s32[]{:T(128)S(6)} %select_n.224), kind=kOutput, calls=%fused_computation.8.clone.1 | convolution fusion | flops 1077936128 | bytes 8912900 | tf_op jit(solution)/shard_map/while/body/eval_jaxpr/scq,skcd->skqd/dot_general | solution.py:54
  252.0 7.3 %fusion.81 = f32[32,256,256]{1,2,0:T(8,128)S(1)} fusion(bf16[32,256,256]{1,2,0:T(8,128)(2,1)S(1)} %bitcast.124, f32[]{:T(128)} %get-tuple-element.704, f32[]{:T(128)} %get-tuple-element.701, f32[]{:T(128)} %get-tuple-element.699, f32[]{:T(128)} %get-tuple-element.697, f32[]{:T(128)} %get-tuple-element.695, f32[]{:T(128)} %get-tuple-element.694, ...), kind=kOutput, calls=%fused_computation.23.clone.1 | convolution fusion | flops 1075904512 | bytes 12589092 | tf_op jit(solution)/shard_map/while/body/eval_jaxpr/qa,nab->nqb/dot_general | solution.py:37
  259.4 8.6 %fusion.82 = f32[32,256]{1,0:T(8,128)S(1)} fusion(f32[32,256,256]{1,2,0:T(8,128)S(1)} %fusion.81, bf16[32,256,256]{1,2,0:T(8,128)(2,1)S(1)} %bitcast.125, f32[]{:T(128)} %get-tuple-element.713, f32[]{:T(128)} %get-tuple-element.712, f32[]{:T(128)} %get-tuple-element.711, f32[]{:T(128)} %get-tuple-element.710, f32[]{:T(128)} %get-tuple-element.709, ...), kind=kOutput, calls=%fused_computation.7.clone.1 | convolution fusion | flops 1080090624 | bytes 12621860 | tf_op jit(solution)/shard_map/while/body/eval_jaxpr/nqa,ba->nqb/dot_general | solution.py:38
  268.2 0.6 dynamic_slice.35
  270.6 5.0 %gather_fusion = bf16[32,256,256]{2,1,0:T(8,128)(2,1)} fusion(bf16[32,256,256]{2,1,0:T(8,128)(2,1)} %get-tuple-element.688, s32[1024]{0:T(1024)S(1)} %pad_clamp_fusion.2), kind=kCustom, calls=%fused_computation.clone.clone.clone.1 | custom fusion | bytes 8388736 | tf_op jit(solution)/shard_map/while/body/eval_jaxpr/gather | solution.py:53
  275.6 4.0 %maximum_convert_fusion.2 = bf16[4,8,256,256]{3,2,1,0:T(8,128)(2,1)S(1)} fusion(bf16[4,8,256,256]{3,2,1,0:T(8,128)(2,1)} %bitcast.126, bf16[32,1,256,256]{3,2,0,1:T(8,128)(2,1)} %get-tuple-element.689, s32[]{:T(128)S(6)} %select_n.224), kind=kOutput, calls=%fused_computation.8.clone.1 | convolution fusion | flops 1077936128 | bytes 8912900 | tf_op jit(solution)/shard_map/while/body/eval_jaxpr/scq,skcd->skqd/dot_general | solution.py:54
  279.6 7.3 %fusion.81 = f32[32,256,256]{1,2,0:T(8,128)S(1)} fusion(bf16[32,256,256]{1,2,0:T(8,128)(2,1)S(1)} %bitcast.124, f32[]{:T(128)} %get-tuple-element.704, f32[]{:T(128)} %get-tuple-element.701, f32[]{:T(128)} %get-tuple-element.699, f32[]{:T(128)} %get-tuple-element.697, f32[]{:T(128)} %get-tuple-element.695, f32[]{:T(128)} %get-tuple-element.694, ...), kind=kOutput, calls=%fused_computation.23.clone.1 | convolution fusion | flops 1075904512 | bytes 12589092 | tf_op jit(solution)/shard_map/while/body/eval_jaxpr/qa,nab->nqb/dot_general | solution.py:37
  286.9 8.6 %fusion.82 = f32[32,256]{1,0:T(8,128)S(1)} fusion(f32[32,256,256]{1,2,0:T(8,128)S(1)} %fusion.81, bf16[32,256,256]{1,2,0:T(8,128)(2,1)S(1)} %bitcast.125, f32[]{:T(128)} %get-tuple-element.713, f32[]{:T(128)} %get-tuple-element.712, f32[]{:T(128)} %get-tuple-element.711, f32[]{:T(128)} %get-tuple-element.710, f32[]{:T(128)} %get-tuple-element.709, ...), kind=kOutput, calls=%fused_computation.7.clone.1 | convolution fusion | flops 1080090624 | bytes 12621860 | tf_op jit(solution)/shard_map/while/body/eval_jaxpr/nqa,ba->nqb/dot_general | solution.py:38
  295.6 0.1 reduce_sum.48
  295.8 10.4 %all_to_all.17 = f32[32,1,8]{2,1,0:T(1,128)S(1)} all-to-all(f32[32,1,8]{2,1,0:T(1,128)S(1)} %bitcast.131), channel_id=1, replica_groups=mesh['db'=8,'pb'=4] {'db','pb'}, dimensions={0} | all-to-all | bytes 2048 | tf_op jit(solution)/shard_map/all_to_all | solution.py:100
  306.2 1.3 gather_fusion.1
  307.5 2.6 top_k.9
  (66 shorter events, 1.8 us)
Async XLA Ops:
  7.2 68.2 %all-gather.2.cloned.1.call-start = ((), (), s32[]{:S(2)}) async-start(), calls=%async_computation.2 | async-start | bytes 4325376 | tf_op jit(solution)/shard_map/all_gather | solution.py:92
  25.2 16.9 %all-to-all-start = ((s32[2,32,8]{2,0,1:T(2,128)}), s32[2,32,8]{2,0,1:T(2,128)S(1)}, u32[]{:S(2)}, u32[]{:S(2)}) async-start(s32[2,32,8]{2,0,1:T(2,128)} %copy.23), calls=%async_computation | async-start | bytes 65536 | tf_op jit(solution)/shard_map/all_to_all | solution.py:95
  32.5 6.5 %copy-start = (bf16[32,256,256]{2,1,0:T(8,128)(2,1)S(1)}, bf16[32,256,256]{2,1,0:T(8,128)(2,1)}, u32[]{:S(2)}) copy-start(bf16[32,256,256]{2,1,0:T(8,128)(2,1)} %param.8) | copy-start | bytes 12582916
  307.5 2.7 copy-start.1
Sparse Core Ops, SparseCore 0:
  11.0 64.3 all-gather.1
where the time goes:
time: 319 us; the launch traced here: 317 us
  matrix products  160 us (50%)
  local copies, waits for them, and re-layouts  63.6 us (20%)
  waiting for transfers between devices  33.2 us (10%)
  other arithmetic  14.3 us (4%)
  between operations  14.2 us (4%)
  loops' own time  14 us (4%)
  blocking collectives  10.4 us (3%)
  starting transfers between devices  7.36 us (2%)
    dot_general x8, matrix products, finish_pairs(): jnp.einsum('nqa,ba->nqb', rectified, conv_db, preferred_element_type=jnp....  69.1 us
    dot_general x8, matrix products, finish_pairs(): jnp.einsum('qa,nab->nqb', conv_query, rectified, preferred_element_type=j...  58.8 us
    gather x8, local copies, waits for them, and re-layouts, score_block(): images = db_unit[slot_block]  39.8 us
    all_gather x1, waiting for transfers between devices, body(): gathered = lax.all_gather(query_unit, ('db', 'pb'), axis=0, tiled=True)  33.2 us
    dot_general x8, matrix products, score_block(): jnp.einsum('scq,skcd->skqd', group_block[:, 0], images, preferred_element...  32.1 us
    another operation x1, loops' own time, shard_scores(): return lax.map(score_block, starts).reshape(source_count, width)  14 us
    all_to_all x1, blocking collectives, body(): lax.all_to_all(found, ('db', 'pb'), split_axis=0, concat_axis=0, tiled=True)  10.4 us
    all_to_all x1, starting transfers between devices, body(): lax.all_to_all(requests, ('db', 'pb'), split_axis=1, concat_axis=1, tiled...  7.33 us
  transfers between devices with their start and end apart: 2, of which 1 were waited for; matrix products, arithmetic and copies ran while one was open for 8% of the time, Pallas kernels for 0%

commit v1 on v0

--- a/solution.py
+++ b/solution.py
@@ -89,7 +89,10 @@
     send_slot = empty.at[shard_of, bucket_pos].set(slot_of)
     send_query = empty.at[shard_of, bucket_pos].set(query_of)
     requests = jnp.stack([send_slot, send_query])
-    gathered = lax.all_gather(query_unit, ("db", "pb"), axis=0, tiled=True)
+    gathered = jnp.concatenate(
+        lax.all_to_all(jnp.stack([query_unit] * lax.axis_size(("db", "pb"))), ("db", "pb"), 0, 0),
+        axis=0,
+    )
     found = shard_scores(
         gathered,
         lax.all_to_all(requests, ("db", "pb"), split_axis=1, concat_axis=1, tiled=True)[0],

time: 319 us -> 368 us (1.15)
  waiting for transfers between devices: 33.2 us -> 90 us
  between operations: 14.2 us -> 0.83 us
    all_to_all x0 -> x1, waiting for transfers between devices: none -> 84.6 us  [body(): lax.all_to_all(jnp.stack([query_unit] * lax.axis_size(('db', 'pb'))), ('d...]
    all_gather x1 -> x0, waiting for transfers between devices: 33.2 us -> none  [body(): gathered = lax.all_gather(query_unit, ('db', 'pb'), axis=0, tiled=True)]
    all_to_all x1, waiting for transfers between devices: 0.01 us -> 5.4 us  [body(): lax.all_to_all(requests, ('db', 'pb'), split_axis=1, concat_axis=1, tiled...]
    all_to_all x0 -> x1, starting transfers between devices: none -> 3.7 us  [body(): lax.all_to_all(jnp.stack([query_unit] * lax.axis_size(('db', 'pb'))), ('d...]
  transfers between devices with their start and end apart: 2 -> 2, of which waited for: 1 -> 2; matrix products, arithmetic and copies ran while one was open for 8% -> 3% of each run, Pallas kernels for 0% -> 0%
where the time goes in v1:
time: 368 us; the launch traced here: 366 us
  matrix products  160 us (43%)
  waiting for transfers between devices  90 us (24%)
  local copies, waits for them, and re-layouts  64 us (17%)
  loops' own time  14 us (4%)
  other arithmetic  13.6 us (4%)
  blocking collectives  12.5 us (3%)
  starting transfers between devices  11 us (3%)
    all_to_all x1, waiting for transfers between devices, body(): lax.all_to_all(jnp.stack([query_unit] * lax.axis_size(('db', 'pb'))), ('d...  84.6 us
    dot_general x8, matrix products, finish_pairs(): jnp.einsum('nqa,ba->nqb', rectified, conv_db, preferred_element_type=jnp....  69 us
    dot_general x8, matrix products, finish_pairs(): jnp.einsum('qa,nab->nqb', conv_query, rectified, preferred_element_type=j...  58.7 us
    gather x8, local copies, waits for them, and re-layouts, score_block(): images = db_unit[slot_block]  39.8 us
    dot_general x8, matrix products, score_block(): jnp.einsum('scq,skcd->skqd', group_block[:, 0], images, preferred_element...  32.1 us
    another operation x1, loops' own time, shard_scores(): return lax.map(score_block, starts).reshape(source_count, width)  14 us
    all_to_all x1, blocking collectives, body(): lax.all_to_all(found, ('db', 'pb'), split_axis=0, concat_axis=0, tiled=True)  12.5 us
  transfers between devices with their start and end apart: 2, of which 2 were waited for; matrix products, arithmetic and copies ran while one was open for 3% of the time, Pallas kernels for 0%

profile of v1, /device:TPU:0, one launch (start us, length us, event | category | flops | bytes accessed | tf_op | source)
XLA Modules:
  0.0 365.8 jit_solution(1738204758392143371)
XLA Ops:
  0.6 0.7 and_select_fusion.3
  1.4 0.2 reduce_window_sum.11
  1.6 0.2 select_reduce_fusion
  1.7 0.7 fusion.62
  2.5 6.4 %scatter_fusion = s32[32,8]{0,1:T(8,128)S(1)} fusion(s32[32,8]{0,1:T(8,128)S(1)} %broadcast_in_dim.11.clone.1, s32[128]{0:T(128)S(1)} %fusion.61, s32[128]{0:T(128)S(1)} %get-tuple-element.487), kind=kCustom, calls=%fused_computation.2 | custom fusion | bytes 2560 | tf_op jit(solution)/shard_map/scatter | solution.py:89
  8.9 6.4 %scatter_fusion.1 = s32[32,8]{0,1:T(8,128)S(1)} fusion(s32[32,8]{0,1:T(8,128)S(1)} %broadcast_in_dim.11.clone, s32[128]{0:T(128)S(1)} %fusion.61, s32[128]{0:T(128)S(1)} %and_select_fusion.2), kind=kCustom, calls=%fused_computation.3 | custom fusion | bytes 2560 | tf_op jit(solution)/shard_map/scatter | solution.py:90
  15.4 0.7 copy.24
  16.0 7.3 %all-to-all-start = ((s32[2,32,8]{2,0,1:T(2,128)}), s32[2,32,8]{2,0,1:T(2,128)S(1)}, u32[]{:S(2)}, u32[]{:S(2)}) async-start(s32[2,32,8]{2,0,1:T(2,128)} %copy.24), calls=%async_computation | async-start | bytes 65536 | tf_op jit(solution)/shard_map/all_to_all | solution.py:98
  23.4 1.0 fusion.53
  24.3 0.9 fusion.55
  25.3 5.4 %all-to-all-done = s32[2,32,8]{2,0,1:T(2,128)S(1)} async-done(((s32[2,32,8]{2,0,1:T(2,128)}), s32[2,32,8]{2,0,1:T(2,128)S(1)}, u32[]{:S(2)}, u32[]{:S(2)}) %all-to-all-start) | async-done | bytes 2080 | tf_op jit(solution)/shard_map/all_to_all | solution.py:98
  30.7 2.4 stack.11
  33.1 3.7 %all-to-all-start.1 = ((bf16[32,1,256,256]{3,2,1,0:T(8,128)(2,1)}), bf16[32,1,256,256]{3,2,1,0:T(8,128)(2,1)}, u32[]{:S(2)}, u32[]{:S(2)}) async-start(bf16[32,1,256,256]{3,2,1,0:T(8,128)(2,1)} %stack.11), calls=%async_computation.1 | async-start | bytes 8388608 | tf_op jit(solution)/shard_map/all_to_all | solution.py:93
  36.9 0.7 fusion.64
  37.6 0.7 fusion.63
  38.3 3.1 fusion.51
  41.4 3.0 fusion.52
  44.4 84.6 %all-to-all-done.1 = bf16[32,1,256,256]{3,2,1,0:T(8,128)(2,1)} async-done(((bf16[32,1,256,256]{3,2,1,0:T(8,128)(2,1)}), bf16[32,1,256,256]{3,2,1,0:T(8,128)(2,1)}, u32[]{:S(2)}, u32[]{:S(2)}) %all-to-all-start.1) | async-done | bytes 4194336 | tf_op jit(solution)/shard_map/all_to_all | solution.py:93
  129.0 220.2 %while.14 = (s32[]{:T(128)}, f32[8,32]{1,0:T(8,128)S(1)}, s32[8]{0:T(128)S(1)}, s32[32,8]{1,0:T(8,128)S(1)}, bf16[32,256,256]{2,1,0:T(8,128)(2,1)}, /*index=5*/b...) while((s32[]{:T(128)}, f32[8,32]{1,0:T(8,128)S(1)}, ...), condition=%wide.region_9.10_spmd.clone.clone, body=%wide.region_6.9_spmd.clone.clone.sunk | while | flops 3233940480 | bytes 42551080 | solution.py:63
  129.0 0.6 dynamic_slice.35
  131.4 5.0 %gather_fusion = bf16[32,256,256]{2,1,0:T(8,128)(2,1)} fusion(bf16[32,256,256]{2,1,0:T(8,128)(2,1)} %get-tuple-element.748, s32[1024]{0:T(1024)S(1)} %pad_clamp_fusion.2), kind=kCustom, calls=%fused_computation.clone.clone.clone.1 | custom fusion | bytes 8388736 | tf_op jit(solution)/shard_map/while/body/eval_jaxpr/gather | solution.py:53
  136.4 4.0 %maximum_convert_fusion.2 = bf16[4,8,256,256]{3,2,1,0:T(8,128)(2,1)S(1)} fusion(bf16[4,8,256,256]{3,2,1,0:T(8,128)(2,1)} %bitcast.128, bf16[32,1,256,256]{3,2,0,1:T(8,128)(2,1)} %get-tuple-element.749, s32[]{:T(128)S(6)} %select_n.224), kind=kOutput, calls=%fused_computation.8.clone.1 | convolution fusion | flops 1077936128 | bytes 8912900 | tf_op jit(solution)/shard_map/while/body/eval_jaxpr/scq,skcd->skqd/dot_general | solution.py:54
  140.4 7.3 %fusion.82 = f32[32,256,256]{1,2,0:T(8,128)S(1)} fusion(bf16[32,256,256]{1,2,0:T(8,128)(2,1)S(1)} %bitcast.126, f32[]{:T(128)} %get-tuple-element.764, f32[]{:T(128)} %get-tuple-element.761, f32[]{:T(128)} %get-tuple-element.759, f32[]{:T(128)} %get-tuple-element.757, f32[]{:T(128)} %get-tuple-element.755, f32[]{:T(128)} %get-tuple-element.754, ...), kind=kOutput, calls=%fused_computation.23.clone.1 | convolution fusion | flops 1075904512 | bytes 12589092 | tf_op jit(solution)/shard_map/while/body/eval_jaxpr/qa,nab->nqb/dot_general | solution.py:37
  147.8 8.6 %fusion.83 = f32[32,256]{1,0:T(8,128)S(1)} fusion(f32[32,256,256]{1,2,0:T(8,128)S(1)} %fusion.82, bf16[32,256,256]{1,2,0:T(8,128)(2,1)S(1)} %bitcast.127, f32[]{:T(128)} %get-tuple-element.773, f32[]{:T(128)} %get-tuple-element.772, f32[]{:T(128)} %get-tuple-element.771, f32[]{:T(128)} %get-tuple-element.770, f32[]{:T(128)} %get-tuple-element.769, ...), kind=kOutput, calls=%fused_computation.7.clone.1 | convolution fusion | flops 1080090624 | bytes 12621860 | tf_op jit(solution)/shard_map/while/body/eval_jaxpr/nqa,ba->nqb/dot_general | solution.py:38
  156.4 0.1 reduce_sum.48
  156.5 0.6 dynamic_slice.35
  158.9 5.0 %gather_fusion = bf16[32,256,256]{2,1,0:T(8,128)(2,1)} fusion(bf16[32,256,256]{2,1,0:T(8,128)(2,1)} %get-tuple-element.748, s32[1024]{0:T(1024)S(1)} %pad_clamp_fusion.2), kind=kCustom, calls=%fused_computation.clone.clone.clone.1 | custom fusion | bytes 8388736 | tf_op jit(solution)/shard_map/while/body/eval_jaxpr/gather | solution.py:53
  163.9 4.0 %maximum_convert_fusion.2 = bf16[4,8,256,256]{3,2,1,0:T(8,128)(2,1)S(1)} fusion(bf16[4,8,256,256]{3,2,1,0:T(8,128)(2,1)} %bitcast.128, bf16[32,1,256,256]{3,2,0,1:T(8,128)(2,1)} %get-tuple-element.749, s32[]{:T(128)S(6)} %select_n.224), kind=kOutput, calls=%fused_computation.8.clone.1 | convolution fusion | flops 1077936128 | bytes 8912900 | tf_op jit(solution)/shard_map/while/body/eval_jaxpr/scq,skcd->skqd/dot_general | solution.py:54
  167.9 7.3 %fusion.82 = f32[32,256,256]{1,2,0:T(8,128)S(1)} fusion(bf16[32,256,256]{1,2,0:T(8,128)(2,1)S(1)} %bitcast.126, f32[]{:T(128)} %get-tuple-element.764, f32[]{:T(128)} %get-tuple-element.761, f32[]{:T(128)} %get-tuple-element.759, f32[]{:T(128)} %get-tuple-element.757, f32[]{:T(128)} %get-tuple-element.755, f32[]{:T(128)} %get-tuple-element.754, ...), kind=kOutput, calls=%fused_computation.23.clone.1 | convolution fusion | flops 1075904512 | bytes 12589092 | tf_op jit(solution)/shard_map/while/body/eval_jaxpr/qa,nab->nqb/dot_general | solution.py:37
  175.3 8.6 %fusion.83 = f32[32,256]{1,0:T(8,128)S(1)} fusion(f32[32,256,256]{1,2,0:T(8,128)S(1)} %fusion.82, bf16[32,256,256]{1,2,0:T(8,128)(2,1)S(1)} %bitcast.127, f32[]{:T(128)} %get-tuple-element.773, f32[]{:T(128)} %get-tuple-element.772, f32[]{:T(128)} %get-tuple-element.771, f32[]{:T(128)} %get-tuple-element.770, f32[]{:T(128)} %get-tuple-element.769, ...), kind=kOutput, calls=%fused_computation.7.clone.1 | convolution fusion | flops 1080090624 | bytes 12621860 | tf_op jit(solution)/shard_map/while/body/eval_jaxpr/nqa,ba->nqb/dot_general | solution.py:38
  183.9 0.1 reduce_sum.48
  184.1 0.6 dynamic_slice.35
  186.5 5.0 %gather_fusion = bf16[32,256,256]{2,1,0:T(8,128)(2,1)} fusion(bf16[32,256,256]{2,1,0:T(8,128)(2,1)} %get-tuple-element.748, s32[1024]{0:T(1024)S(1)} %pad_clamp_fusion.2), kind=kCustom, calls=%fused_computation.clone.clone.clone.1 | custom fusion | bytes 8388736 | tf_op jit(solution)/shard_map/while/body/eval_jaxpr/gather | solution.py:53
  191.4 4.0 %maximum_convert_fusion.2 = bf16[4,8,256,256]{3,2,1,0:T(8,128)(2,1)S(1)} fusion(bf16[4,8,256,256]{3,2,1,0:T(8,128)(2,1)} %bitcast.128, bf16[32,1,256,256]{3,2,0,1:T(8,128)(2,1)} %get-tuple-element.749, s32[]{:T(128)S(6)} %select_n.224), kind=kOutput, calls=%fused_computation.8.clone.1 | convolution fusion | flops 1077936128 | bytes 8912900 | tf_op jit(solution)/shard_map/while/body/eval_jaxpr/scq,skcd->skqd/dot_general | solution.py:54
  195.5 7.3 %fusion.82 = f32[32,256,256]{1,2,0:T(8,128)S(1)} fusion(bf16[32,256,256]{1,2,0:T(8,128)(2,1)S(1)} %bitcast.126, f32[]{:T(128)} %get-tuple-element.764, f32[]{:T(128)} %get-tuple-element.761, f32[]{:T(128)} %get-tuple-element.759, f32[]{:T(128)} %get-tuple-element.757, f32[]{:T(128)} %get-tuple-element.755, f32[]{:T(128)} %get-tuple-element.754, ...), kind=kOutput, calls=%fused_computation.23.clone.1 | convolution fusion | flops 1075904512 | bytes 12589092 | tf_op jit(solution)/shard_map/while/body/eval_jaxpr/qa,nab->nqb/dot_general | solution.py:37
  202.8 8.6 %fusion.83 = f32[32,256]{1,0:T(8,128)S(1)} fusion(f32[32,256,256]{1,2,0:T(8,128)S(1)} %fusion.82, bf16[32,256,256]{1,2,0:T(8,128)(2,1)S(1)} %bitcast.127, f32[]{:T(128)} %get-tuple-element.773, f32[]{:T(128)} %get-tuple-element.772, f32[]{:T(128)} %get-tuple-element.771, f32[]{:T(128)} %get-tuple-element.770, f32[]{:T(128)} %get-tuple-element.769, ...), kind=kOutput, calls=%fused_computation.7.clone.1 | convolution fusion | flops 1080090624 | bytes 12621860 | tf_op jit(solution)/shard_map/while/body/eval_jaxpr/nqa,ba->nqb/dot_general | solution.py:38
  211.6 0.6 dynamic_slice.35
  214.0 5.0 %gather_fusion = bf16[32,256,256]{2,1,0:T(8,128)(2,1)} fusion(bf16[32,256,256]{2,1,0:T(8,128)(2,1)} %get-tuple-element.748, s32[1024]{0:T(1024)S(1)} %pad_clamp_fusion.2), kind=kCustom, calls=%fused_computation.clone.clone.clone.1 | custom fusion | bytes 8388736 | tf_op jit(solution)/shard_map/while/body/eval_jaxpr/gather | solution.py:53
  219.0 4.0 %maximum_convert_fusion.2 = bf16[4,8,256,256]{3,2,1,0:T(8,128)(2,1)S(1)} fusion(bf16[4,8,256,256]{3,2,1,0:T(8,128)(2,1)} %bitcast.128, bf16[32,1,256,256]{3,2,0,1:T(8,128)(2,1)} %get-tuple-element.749, s32[]{:T(128)S(6)} %select_n.224), kind=kOutput, calls=%fused_computation.8.clone.1 | convolution fusion | flops 1077936128 | bytes 8912900 | tf_op jit(solution)/shard_map/while/body/eval_jaxpr/scq,skcd->skqd/dot_general | solution.py:54
  223.0 7.3 %fusion.82 = f32[32,256,256]{1,2,0:T(8,128)S(1)} fusion(bf16[32,256,256]{1,2,0:T(8,128)(2,1)S(1)} %bitcast.126, f32[]{:T(128)} %get-tuple-element.764, f32[]{:T(128)} %get-tuple-element.761, f32[]{:T(128)} %get-tuple-element.759, f32[]{:T(128)} %get-tuple-element.757, f32[]{:T(128)} %get-tuple-element.755, f32[]{:T(128)} %get-tuple-element.754, ...), kind=kOutput, calls=%fused_computation.23.clone.1 | convolution fusion | flops 1075904512 | bytes 12589092 | tf_op jit(solution)/shard_map/while/body/eval_jaxpr/qa,nab->nqb/dot_general | solution.py:37
  230.3 8.6 %fusion.83 = f32[32,256]{1,0:T(8,128)S(1)} fusion(f32[32,256,256]{1,2,0:T(8,128)S(1)} %fusion.82, bf16[32,256,256]{1,2,0:T(8,128)(2,1)S(1)} %bitcast.127, f32[]{:T(128)} %get-tuple-element.773, f32[]{:T(128)} %get-tuple-element.772, f32[]{:T(128)} %get-tuple-element.771, f32[]{:T(128)} %get-tuple-element.770, f32[]{:T(128)} %get-tuple-element.769, ...), kind=kOutput, calls=%fused_computation.7.clone.1 | convolution fusion | flops 1080090624 | bytes 12621860 | tf_op jit(solution)/shard_map/while/body/eval_jaxpr/nqa,ba->nqb/dot_general | solution.py:38
  239.1 0.6 dynamic_slice.35
  241.5 5.0 %gather_fusion = bf16[32,256,256]{2,1,0:T(8,128)(2,1)} fusion(bf16[32,256,256]{2,1,0:T(8,128)(2,1)} %get-tuple-element.748, s32[1024]{0:T(1024)S(1)} %pad_clamp_fusion.2), kind=kCustom, calls=%fused_computation.clone.clone.clone.1 | custom fusion | bytes 8388736 | tf_op jit(solution)/shard_map/while/body/eval_jaxpr/gather | solution.py:53
  246.5 4.0 %maximum_convert_fusion.2 = bf16[4,8,256,256]{3,2,1,0:T(8,128)(2,1)S(1)} fusion(bf16[4,8,256,256]{3,2,1,0:T(8,128)(2,1)} %bitcast.128, bf16[32,1,256,256]{3,2,0,1:T(8,128)(2,1)} %get-tuple-element.749, s32[]{:T(128)S(6)} %select_n.224), kind=kOutput, calls=%fused_computation.8.clone.1 | convolution fusion | flops 1077936128 | bytes 8912900 | tf_op jit(solution)/shard_map/while/body/eval_jaxpr/scq,skcd->skqd/dot_general | solution.py:54
  250.5 7.3 %fusion.82 = f32[32,256,256]{1,2,0:T(8,128)S(1)} fusion(bf16[32,256,256]{1,2,0:T(8,128)(2,1)S(1)} %bitcast.126, f32[]{:T(128)} %get-tuple-element.764, f32[]{:T(128)} %get-tuple-element.761, f32[]{:T(128)} %get-tuple-element.759, f32[]{:T(128)} %get-tuple-element.757, f32[]{:T(128)} %get-tuple-element.755, f32[]{:T(128)} %get-tuple-element.754, ...), kind=kOutput, calls=%fused_computation.23.clone.1 | convolution fusion | flops 1075904512 | bytes 12589092 | tf_op jit(solution)/shard_map/while/body/eval_jaxpr/qa,nab->nqb/dot_general | solution.py:37
  257.9 8.6 %fusion.83 = f32[32,256]{1,0:T(8,128)S(1)} fusion(f32[32,256,256]{1,2,0:T(8,128)S(1)} %fusion.82, bf16[32,256,256]{1,2,0:T(8,128)(2,1)S(1)} %bitcast.127, f32[]{:T(128)} %get-tuple-element.773, f32[]{:T(128)} %get-tuple-element.772, f32[]{:T(128)} %get-tuple-element.771, f32[]{:T(128)} %get-tuple-element.770, f32[]{:T(128)} %get-tuple-element.769, ...), kind=kOutput, calls=%fused_computation.7.clone.1 | convolution fusion | flops 1080090624 | bytes 12621860 | tf_op jit(solution)/shard_map/while/body/eval_jaxpr/nqa,ba->nqb/dot_general | solution.py:38
  266.7 0.6 dynamic_slice.35
  269.0 5.0 %gather_fusion = bf16[32,256,256]{2,1,0:T(8,128)(2,1)} fusion(bf16[32,256,256]{2,1,0:T(8,128)(2,1)} %get-tuple-element.748, s32[1024]{0:T(1024)S(1)} %pad_clamp_fusion.2), kind=kCustom, calls=%fused_computation.clone.clone.clone.1 | custom fusion | bytes 8388736 | tf_op jit(solution)/shard_map/while/body/eval_jaxpr/gather | solution.py:53
  274.0 4.0 %maximum_convert_fusion.2 = bf16[4,8,256,256]{3,2,1,0:T(8,128)(2,1)S(1)} fusion(bf16[4,8,256,256]{3,2,1,0:T(8,128)(2,1)} %bitcast.128, bf16[32,1,256,256]{3,2,0,1:T(8,128)(2,1)} %get-tuple-element.749, s32[]{:T(128)S(6)} %select_n.224), kind=kOutput, calls=%fused_computation.8.clone.1 | convolution fusion | flops 1077936128 | bytes 8912900 | tf_op jit(solution)/shard_map/while/body/eval_jaxpr/scq,skcd->skqd/dot_general | solution.py:54
  278.0 7.3 %fusion.82 = f32[32,256,256]{1,2,0:T(8,128)S(1)} fusion(bf16[32,256,256]{1,2,0:T(8,128)(2,1)S(1)} %bitcast.126, f32[]{:T(128)} %get-tuple-element.764, f32[]{:T(128)} %get-tuple-element.761, f32[]{:T(128)} %get-tuple-element.759, f32[]{:T(128)} %get-tuple-element.757, f32[]{:T(128)} %get-tuple-element.755, f32[]{:T(128)} %get-tuple-element.754, ...), kind=kOutput, calls=%fused_computation.23.clone.1 | convolution fusion | flops 1075904512 | bytes 12589092 | tf_op jit(solution)/shard_map/while/body/eval_jaxpr/qa,nab->nqb/dot_general | solution.py:37
  285.4 8.6 %fusion.83 = f32[32,256]{1,0:T(8,128)S(1)} fusion(f32[32,256,256]{1,2,0:T(8,128)S(1)} %fusion.82, bf16[32,256,256]{1,2,0:T(8,128)(2,1)S(1)} %bitcast.127, f32[]{:T(128)} %get-tuple-element.773, f32[]{:T(128)} %get-tuple-element.772, f32[]{:T(128)} %get-tuple-element.771, f32[]{:T(128)} %get-tuple-element.770, f32[]{:T(128)} %get-tuple-element.769, ...), kind=kOutput, calls=%fused_computation.7.clone.1 | convolution fusion | flops 1080090624 | bytes 12621860 | tf_op jit(solution)/shard_map/while/body/eval_jaxpr/nqa,ba->nqb/dot_general | solution.py:38
  294.2 0.6 dynamic_slice.35
  296.6 5.0 %gather_fusion = bf16[32,256,256]{2,1,0:T(8,128)(2,1)} fusion(bf16[32,256,256]{2,1,0:T(8,128)(2,1)} %get-tuple-element.748, s32[1024]{0:T(1024)S(1)} %pad_clamp_fusion.2), kind=kCustom, calls=%fused_computation.clone.clone.clone.1 | custom fusion | bytes 8388736 | tf_op jit(solution)/shard_map/while/body/eval_jaxpr/gather | solution.py:53
  301.6 4.0 %maximum_convert_fusion.2 = bf16[4,8,256,256]{3,2,1,0:T(8,128)(2,1)S(1)} fusion(bf16[4,8,256,256]{3,2,1,0:T(8,128)(2,1)} %bitcast.128, bf16[32,1,256,256]{3,2,0,1:T(8,128)(2,1)} %get-tuple-element.749, s32[]{:T(128)S(6)} %select_n.224), kind=kOutput, calls=%fused_computation.8.clone.1 | convolution fusion | flops 1077936128 | bytes 8912900 | tf_op jit(solution)/shard_map/while/body/eval_jaxpr/scq,skcd->skqd/dot_general | solution.py:54
  305.6 7.3 %fusion.82 = f32[32,256,256]{1,2,0:T(8,128)S(1)} fusion(bf16[32,256,256]{1,2,0:T(8,128)(2,1)S(1)} %bitcast.126, f32[]{:T(128)} %get-tuple-element.764, f32[]{:T(128)} %get-tuple-element.761, f32[]{:T(128)} %get-tuple-element.759, f32[]{:T(128)} %get-tuple-element.757, f32[]{:T(128)} %get-tuple-element.755, f32[]{:T(128)} %get-tuple-element.754, ...), kind=kOutput, calls=%fused_computation.23.clone.1 | convolution fusion | flops 1075904512 | bytes 12589092 | tf_op jit(solution)/shard_map/while/body/eval_jaxpr/qa,nab->nqb/dot_general | solution.py:37
  312.9 8.6 %fusion.83 = f32[32,256]{1,0:T(8,128)S(1)} fusion(f32[32,256,256]{1,2,0:T(8,128)S(1)} %fusion.82, bf16[32,256,256]{1,2,0:T(8,128)(2,1)S(1)} %bitcast.127, f32[]{:T(128)} %get-tuple-element.773, f32[]{:T(128)} %get-tuple-element.772, f32[]{:T(128)} %get-tuple-element.771, f32[]{:T(128)} %get-tuple-element.770, f32[]{:T(128)} %get-tuple-element.769, ...), kind=kOutput, calls=%fused_computation.7.clone.1 | convolution fusion | flops 1080090624 | bytes 12621860 | tf_op jit(solution)/shard_map/while/body/eval_jaxpr/nqa,ba->nqb/dot_general | solution.py:38
  321.7 0.6 dynamic_slice.35
  324.1 5.0 %gather_fusion = bf16[32,256,256]{2,1,0:T(8,128)(2,1)} fusion(bf16[32,256,256]{2,1,0:T(8,128)(2,1)} %get-tuple-element.748, s32[1024]{0:T(1024)S(1)} %pad_clamp_fusion.2), kind=kCustom, calls=%fused_computation.clone.clone.clone.1 | custom fusion | bytes 8388736 | tf_op jit(solution)/shard_map/while/body/eval_jaxpr/gather | solution.py:53
  329.1 4.0 %maximum_convert_fusion.2 = bf16[4,8,256,256]{3,2,1,0:T(8,128)(2,1)S(1)} fusion(bf16[4,8,256,256]{3,2,1,0:T(8,128)(2,1)} %bitcast.128, bf16[32,1,256,256]{3,2,0,1:T(8,128)(2,1)} %get-tuple-element.749, s32[]{:T(128)S(6)} %select_n.224), kind=kOutput, calls=%fused_computation.8.clone.1 | convolution fusion | flops 1077936128 | bytes 8912900 | tf_op jit(solution)/shard_map/while/body/eval_jaxpr/scq,skcd->skqd/dot_general | solution.py:54
  333.1 7.3 %fusion.82 = f32[32,256,256]{1,2,0:T(8,128)S(1)} fusion(bf16[32,256,256]{1,2,0:T(8,128)(2,1)S(1)} %bitcast.126, f32[]{:T(128)} %get-tuple-element.764, f32[]{:T(128)} %get-tuple-element.761, f32[]{:T(128)} %get-tuple-element.759, f32[]{:T(128)} %get-tuple-element.757, f32[]{:T(128)} %get-tuple-element.755, f32[]{:T(128)} %get-tuple-element.754, ...), kind=kOutput, calls=%fused_computation.23.clone.1 | convolution fusion | flops 1075904512 | bytes 12589092 | tf_op jit(solution)/shard_map/while/body/eval_jaxpr/qa,nab->nqb/dot_general | solution.py:37
  340.4 8.6 %fusion.83 = f32[32,256]{1,0:T(8,128)S(1)} fusion(f32[32,256,256]{1,2,0:T(8,128)S(1)} %fusion.82, bf16[32,256,256]{1,2,0:T(8,128)(2,1)S(1)} %bitcast.127, f32[]{:T(128)} %get-tuple-element.773, f32[]{:T(128)} %get-tuple-element.772, f32[]{:T(128)} %get-tuple-element.771, f32[]{:T(128)} %get-tuple-element.770, f32[]{:T(128)} %get-tuple-element.769, ...), kind=kOutput, calls=%fused_computation.7.clone.1 | convolution fusion | flops 1080090624 | bytes 12621860 | tf_op jit(solution)/shard_map/while/body/eval_jaxpr/nqa,ba->nqb/dot_general | solution.py:38
  349.3 12.5 %all_to_all.22 = f32[32,1,8]{2,1,0:T(1,128)S(1)} all-to-all(f32[32,1,8]{2,1,0:T(1,128)S(1)} %bitcast.132), channel_id=1, replica_groups=mesh['db'=8,'pb'=4] {'db','pb'}, dimensions={0} | all-to-all | bytes 2048 | tf_op jit(solution)/shard_map/all_to_all | solution.py:103
  361.8 1.3 gather_fusion.1
  363.1 2.6 top_k.9
  (70 shorter events, 2.1 us)
Async XLA Ops:
  16.0 14.6 %all-to-all-start = ((s32[2,32,8]{2,0,1:T(2,128)}), s32[2,32,8]{2,0,1:T(2,128)S(1)}, u32[]{:S(2)}, u32[]{:S(2)}) async-start(s32[2,32,8]{2,0,1:T(2,128)} %copy.24), calls=%async_computation | async-start | bytes 65536 | tf_op jit(solution)/shard_map/all_to_all | solution.py:98
  33.1 3.8 %copy-start.1 = (bf16[3,3]{1,0:T(4,128)(2,1)S(1)}, bf16[3,3]{1,0:T(4,128)(2,1)}, u32[]{:S(2)}) copy-start(bf16[3,3]{1,0:T(4,128)(2,1)} %param.10) | copy-start | bytes 58
  33.1 4.5 %copy-start.2 = (bf16[3,3]{1,0:T(4,128)(2,1)S(1)}, bf16[3,3]{1,0:T(4,128)(2,1)}, u32[]{:S(2)}) copy-start(bf16[3,3]{1,0:T(4,128)(2,1)} %param.11) | copy-start | bytes 58
  33.1 95.9 %all-to-all-start.1 = ((bf16[32,1,256,256]{3,2,1,0:T(8,128)(2,1)}), bf16[32,1,256,256]{3,2,1,0:T(8,128)(2,1)}, u32[]{:S(2)}, u32[]{:S(2)}) async-start(bf16[32,1,256,256]{3,2,1,0:T(8,128)(2,1)} %stack.11), calls=%async_computation.1 | async-start | bytes 8388608 | tf_op jit(solution)/shard_map/all_to_all | solution.py:93
  36.8 4.5 %copy-start = (bf16[32,256,256]{2,1,0:T(8,128)(2,1)S(1)}, bf16[32,256,256]{2,1,0:T(8,128)(2,1)}, u32[]{:S(2)}) copy-start(bf16[32,256,256]{2,1,0:T(8,128)(2,1)} %param.8) | copy-start | bytes 12582916
  363.1 2.7 copy-start.3
